TPU v7x, 32 devices: a whole 2x2x4 slice. The times are simulated.
32 devices in a mesh: batch: 8 (over y, x, core), head: 4 (over z).
Axes of the slice: x: 2, y: 2, z: 4, core: 2. Of those that a mesh axis runs over, the one named last changes fastest.
Arguments:
- layer_input: bfloat16 [16384, 768], P(('batch', 'head')), may hold values from -6 to 6
- memory_flags: int32 [32], P('batch'), may hold values 0 or 1
- document_start: int32 [32], P('batch'), may hold values from 1 to 511
- memory_coefficients: bfloat16 [32, 256, 768], P('batch'), may hold values from -6 to 6
- first_gain: bfloat16 [768], replicated, may hold values from 0.5 to 1.5
- first_shift: bfloat16 [768], replicated, may hold values from -1 to 1
- query_weight: bfloat16 [768, 768], P(None, 'head'), may hold values from -0.3125 to 0.3125
- query_bias: bfloat16 [768], P('head'), may hold values from -1 to 1
- key_matrix: bfloat16 [768, 768], P(None, 'head'), may hold values from -0.21875 to 0.21875
- value_matrix: bfloat16 [768, 768], P(None, 'head'), may hold values from -0.21875 to 0.21875
- value_offset_bias: bfloat16 [768], P('head'), may hold values from -1 to 1
- out_weight: bfloat16 [768, 768], P('head'), may hold values from -0.875 to 0.875
- out_bias: bfloat16 [768], replicated, may hold values from -1 to 1
- second_gain: bfloat16 [768], replicated, may hold values from 0.5 to 1.5
- second_shift: bfloat16 [768], replicated, may hold values from -1 to 1
- up_weight: bfloat16 [768, 3072], P(None, 'head'), may hold values from -0.21875 to 0.21875
- up_bias: bfloat16 [3072], P('head'), may hold values from -1 to 1
- down_weight: bfloat16 [3072, 768], P('head'), may hold values from -0.109375 to 0.109375
- down_bias: bfloat16 [768], replicated, may hold values from -1 to 1
- centre_weight: float32 [12, 256], P('head'), may hold values from -0.375 to 0.375
- width_weight: float32 [12, 256], P('head'), may hold values from -0.375 to 0.375
- grad_output: bfloat16 [16384, 768], P(('batch', 'head')), may hold values from -6 to 6
Outputs:
- layer_output: bfloat16 [16384, 768], P(('batch', 'head'))
- input_grad: bfloat16 [16384, 768], P(('batch', 'head'))
- first_gain_grad: float32 [768], replicated
- first_shift_grad: float32 [768], replicated
- query_weight_grad: float32 [768, 768], P(None, 'head')
- query_bias_grad: float32 [768], P('head')
- key_weight_grad: float32 [768, 768], P(None, 'head')
- value_weight_grad: float32 [768, 768], P(None, 'head')
- value_bias_grad: float32 [768], P('head')
- out_weight_grad: float32 [768, 768], P('head')
- out_bias_grad: float32 [768], replicated
- second_gain_grad: float32 [768], replicated
- second_shift_grad: float32 [768], replicated
- up_weight_grad: float32 [768, 3072], P(None, 'head')
- up_bias_grad: float32 [3072], P('head')
- down_weight_grad: float32 [3072, 768], P('head')
- down_bias_grad: float32 [768], replicated
- centre_weight_grad: float32 [12, 256], P('head')
- width_weight_grad: float32 [12, 256], P('head')
Inputs may be any that keep to these rules, and one draw needn't show every extreme that they name: `memory_flags`: 1 marks a segment with memory.
All inputs are finite; a program needn't handle non-finite values. No bound on the sum of `memory_flags` on one device may be relied on, other than what follows from the above.
Results may differ from a plain program's by a relative error of at most 0.018.
The roundings to bfloat16 on the way count: a program that leaves them out, or rounds other values in their place, can miss the bound.
Values may be sent and summed in bfloat16 or wider, within the bound.
A program may use at most 128 MiB of HBM per device.

v0:
```python
import math
import jax
import jax.numpy as jnp
from jax import lax
from jax.sharding import PartitionSpec as P


def norm_stats(values_in):
    center = values_in - jnp.mean(values_in, axis=-1, keepdims=True)
    factor = lax.rsqrt(jnp.mean(center * center, axis=-1, keepdims=True) + 1e-05)
    return (center * factor, factor)


def norm_back(grad, normed, factor):
    return factor * (
        grad
        - jnp.mean(grad, axis=-1, keepdims=True)
        - normed * jnp.mean(grad * normed, axis=-1, keepdims=True)
    )


def cross_dot(left, right):
    return lax.dot_general(
        left, right, (((0,), (0,)), ((), ())), preferred_element_type=jnp.float32
    )


def back_dot(left, right):
    return lax.dot_general(
        left, right, (((1,), (1,)), ((), ())), preferred_element_type=jnp.float32
    )


def segment_mask(length, bound):
    row_ids = lax.broadcasted_iota(jnp.int32, (length, length), 0)
    col_ids = lax.broadcasted_iota(jnp.int32, (length, length), 1)
    return (col_ids <= row_ids) & ((col_ids >= bound) | (row_ids < bound))


def masked_scores(queries, keys_low, bound):
    factor = queries.shape[-1] ** (-0.5)
    scores = (
        jnp.einsum("qhd,khd->hqk", queries, keys_low, preferred_element_type=jnp.float32) * factor
    )
    return jnp.where(segment_mask(queries.shape[0], bound)[None], scores, -1000000000.0)


def recall_terms(queries, memory_keys, centre_weight, width_weight):
    factor = queries.shape[-1] ** (-0.5)
    mem_scores = (
        jnp.einsum("qhd,nhd->hqn", queries, memory_keys, preferred_element_type=jnp.float32)
        * factor
    )
    centre = jax.nn.sigmoid(
        jnp.einsum("hqn,hn->hq", mem_scores, centre_weight, precision=lax.Precision.HIGHEST)
    )
    width_pre = jnp.einsum("hqn,hn->hq", mem_scores, width_weight, precision=lax.Precision.HIGHEST)
    spread = 0.02 * jax.nn.softplus(width_pre) + 0.01
    basis_count = memory_keys.shape[0]
    centres = (jnp.arange(basis_count, dtype=jnp.float32) + 0.5) / basis_count
    offset = centre[..., None] - centres
    recall = (
        jnp.exp(-offset * offset / (2.0 * spread[..., None]))
        * lax.rsqrt(2.0 * math.pi * spread[..., None])
        / basis_count
    )
    return (mem_scores, centre, width_pre, spread, offset, recall)


def forward_segment(segment_item, centre_weight, width_weight):
    queries, keys_low, values, memory_keys, memory_values, flag, bound = segment_item
    scores = masked_scores(queries, keys_low, bound)
    row_peak = jnp.max(scores, axis=-1, keepdims=True)
    shifted = jnp.exp(scores - row_peak)
    row_total = jnp.sum(shifted, axis=-1, keepdims=True)
    probs_low = (shifted / row_total).astype(jnp.bfloat16)
    local_mix = jnp.einsum("hqk,khd->qhd", probs_low, values, preferred_element_type=jnp.float32)
    recall_low = recall_terms(queries, memory_keys, centre_weight, width_weight)[5].astype(
        jnp.bfloat16
    )
    recalled = jnp.einsum(
        "hqn,nhd->qhd", recall_low, memory_values, preferred_element_type=jnp.float32
    )
    context = (local_mix + flag * recalled).astype(jnp.bfloat16)
    return (context, (row_peak + jnp.log(row_total))[..., 0])


def backward_segment(segment_item, centre_weight, width_weight):
    queries, keys_low, values, memory_keys, memory_values, flag, bound, log_total, grad_context = (
        segment_item
    )
    factor = queries.shape[-1] ** (-0.5)
    scores = masked_scores(queries, keys_low, bound)
    attn_probs = jnp.exp(scores - log_total[..., None])
    probs_low = attn_probs.astype(jnp.bfloat16)
    grad_values = jnp.einsum(
        "hqk,qhd->khd", probs_low, grad_context, preferred_element_type=jnp.float32
    )
    grad_probs = jnp.einsum(
        "qhd,khd->hqk", grad_context, values, preferred_element_type=jnp.float32
    )
    grad_scores = (
        attn_probs * (grad_probs - jnp.sum(attn_probs * grad_probs, axis=-1, keepdims=True))
    ).astype(jnp.bfloat16)
    mem_scores, centre, width_pre, spread, offset, recall = recall_terms(
        queries, memory_keys, centre_weight, width_weight
    )
    recall_low = recall.astype(jnp.bfloat16)
    grad_recall = flag * jnp.einsum(
        "qhd,nhd->hqn", grad_context, memory_values, preferred_element_type=jnp.float32
    )
    memory_value_gradient = flag * jnp.einsum(
        "hqn,qhd->nhd", recall_low, grad_context, preferred_element_type=jnp.float32
    )
    weighted = grad_recall * recall
    spread_b = spread[..., None]
    grad_centre = jnp.sum(weighted * (-offset / spread_b), axis=-1)
    grad_spread = jnp.sum(
        weighted * (offset * offset / (2.0 * spread_b * spread_b) - 0.5 / spread_b), axis=-1
    )
    centre_pre_grad = grad_centre * centre * (1.0 - centre)
    width_pre_grad = grad_spread * 0.02 * jax.nn.sigmoid(width_pre)
    grad_mem_scores = (
        centre_pre_grad[..., None] * centre_weight[:, None, :]
        + width_pre_grad[..., None] * width_weight[:, None, :]
    ).astype(jnp.bfloat16)
    centre_grad = jnp.einsum(
        "hq,hqn->hn", centre_pre_grad, mem_scores, precision=lax.Precision.HIGHEST
    )
    width_grad = jnp.einsum(
        "hq,hqn->hn", width_pre_grad, mem_scores, precision=lax.Precision.HIGHEST
    )
    grad_queries = factor * (
        jnp.einsum("hqk,khd->qhd", grad_scores, keys_low, preferred_element_type=jnp.float32)
        + jnp.einsum(
            "hqn,nhd->qhd", grad_mem_scores, memory_keys, preferred_element_type=jnp.float32
        )
    )
    grad_keys = factor * jnp.einsum(
        "hqk,qhd->khd", grad_scores, queries, preferred_element_type=jnp.float32
    )
    memory_key_gradient = factor * jnp.einsum(
        "hqn,qhd->nhd", grad_mem_scores, queries, preferred_element_type=jnp.float32
    )
    return (
        grad_queries.astype(jnp.bfloat16),
        grad_keys.astype(jnp.bfloat16),
        grad_values.astype(jnp.bfloat16),
        memory_key_gradient.astype(jnp.bfloat16),
        memory_value_gradient.astype(jnp.bfloat16),
        centre_grad,
        width_grad,
    )


def per_device(
    layer_input,
    memory_flags,
    document_start,
    memory_coefficients,
    first_gain,
    first_shift,
    query_weight,
    query_bias,
    key_matrix,
    value_matrix,
    value_offset_bias,
    out_weight,
    out_bias,
    second_gain,
    second_shift,
    up_weight,
    up_bias,
    down_weight,
    down_bias,
    centre_weight,
    width_weight,
    grad_output,
):
    segments = memory_coefficients.shape[0]
    basis_count = memory_coefficients.shape[1]
    group_heads = centre_weight.shape[0]
    group_cols = query_weight.shape[1]
    head_size = group_cols // group_heads
    flag_values = memory_flags.astype(jnp.float32)
    inputs = layer_input.astype(jnp.float32)
    normed_one, factor_one = norm_stats(inputs)
    first_low = (normed_one * first_gain + first_shift).astype(jnp.bfloat16)
    first_rows = lax.all_gather(first_low, "head", axis=0, tiled=True)
    total_rows = first_rows.shape[0]
    length = total_rows // segments
    queries = (
        jnp.dot(first_rows, query_weight, preferred_element_type=jnp.float32) + query_bias
    ).astype(jnp.bfloat16)
    keys_low = jnp.dot(first_rows, key_matrix, preferred_element_type=jnp.float32).astype(
        jnp.bfloat16
    )
    values = (
        jnp.dot(first_rows, value_matrix, preferred_element_type=jnp.float32) + value_offset_bias
    ).astype(jnp.bfloat16)
    memory_keys = jnp.einsum(
        "wmr,rq->wmq", memory_coefficients, key_matrix, preferred_element_type=jnp.float32
    ).astype(jnp.bfloat16)
    memory_values = (
        jnp.einsum(
            "wmr,rq->wmq", memory_coefficients, value_matrix, preferred_element_type=jnp.float32
        )
        + value_offset_bias
    ).astype(jnp.bfloat16)
    tile_shape = (segments, length, group_heads, head_size)
    basis_dimensions = (segments, basis_count, group_heads, head_size)
    seg_items = (
        queries.reshape(tile_shape),
        keys_low.reshape(tile_shape),
        values.reshape(tile_shape),
        memory_keys.reshape(basis_dimensions),
        memory_values.reshape(basis_dimensions),
        flag_values,
        document_start,
    )
    context, log_total = lax.map(
        lambda segment_item: forward_segment(segment_item, centre_weight, width_weight), seg_items
    )
    context = context.reshape(total_rows, group_cols)
    attn_sum = lax.psum_scatter(
        jnp.dot(context, out_weight, preferred_element_type=jnp.float32).astype(jnp.bfloat16),
        "head",
        scatter_dimension=0,
        tiled=True,
    ).astype(jnp.float32)
    hidden = inputs + (attn_sum + out_bias)
    normed_two, factor_two = norm_stats(hidden)
    second_low = (normed_two * second_gain + second_shift).astype(jnp.bfloat16)
    second_rows = lax.all_gather(second_low, "head", axis=0, tiled=True)
    up_pre = jnp.dot(second_rows, up_weight, preferred_element_type=jnp.float32) + up_bias
    up_act = jax.nn.gelu(up_pre, approximate=True).astype(jnp.bfloat16)
    mlp_sum = lax.psum_scatter(
        jnp.dot(up_act, down_weight, preferred_element_type=jnp.float32).astype(jnp.bfloat16),
        "head",
        scatter_dimension=0,
        tiled=True,
    ).astype(jnp.float32)
    layer_output = (hidden + (mlp_sum + down_bias)).astype(jnp.bfloat16)
    down_bias_grad = jnp.sum(grad_output.astype(jnp.float32), axis=0)
    grad_rows = lax.all_gather(grad_output, "head", axis=0, tiled=True)
    down_weight_grad = cross_dot(up_act, grad_rows)
    grad_act = back_dot(grad_rows, down_weight)
    gelu_pull = jax.vjp(lambda values_in: jax.nn.gelu(values_in, approximate=True), up_pre)[1]
    grad_up = gelu_pull(grad_act)[0].astype(jnp.bfloat16)
    up_bias_grad = jnp.sum(grad_up.astype(jnp.float32), axis=0)
    up_weight_grad = cross_dot(second_rows, grad_up)
    grad_second = lax.psum_scatter(
        back_dot(grad_up, up_weight).astype(jnp.bfloat16), "head", scatter_dimension=0, tiled=True
    ).astype(jnp.float32)
    second_gain_grad = jnp.sum(grad_second * normed_two, axis=0)
    second_shift_grad = jnp.sum(grad_second, axis=0)
    grad_hidden = grad_output.astype(jnp.float32) + norm_back(
        grad_second * second_gain, normed_two, factor_two
    )
    branch_low = grad_hidden.astype(jnp.bfloat16)
    out_bias_grad = jnp.sum(branch_low.astype(jnp.float32), axis=0)
    branch_rows = lax.all_gather(branch_low, "head", axis=0, tiled=True)
    out_weight_grad = cross_dot(context, branch_rows)
    grad_context = back_dot(branch_rows, out_weight).astype(jnp.bfloat16)
    back_items = seg_items + (log_total, grad_context.reshape(tile_shape))
    results = lax.map(
        lambda segment_item: backward_segment(segment_item, centre_weight, width_weight), back_items
    )
    grad_queries = results[0].reshape(total_rows, group_cols)
    grad_keys = results[1].reshape(total_rows, group_cols)
    grad_values = results[2].reshape(total_rows, group_cols)
    memory_key_gradient = results[3].reshape(segments, basis_count, group_cols)
    memory_value_gradient = results[4].reshape(segments, basis_count, group_cols)
    centre_weight_grad = jnp.sum(results[5], axis=0)
    width_weight_grad = jnp.sum(results[6], axis=0)
    query_weight_grad = cross_dot(first_rows, grad_queries)
    query_bias_grad = jnp.sum(grad_queries.astype(jnp.float32), axis=0)
    key_weight_grad = cross_dot(first_rows, grad_keys) + jnp.einsum(
        "qwo,qwy->oy", memory_coefficients, memory_key_gradient, preferred_element_type=jnp.float32
    )
    value_weight_grad = cross_dot(first_rows, grad_values) + jnp.einsum(
        "qwo,qwy->oy",
        memory_coefficients,
        memory_value_gradient,
        preferred_element_type=jnp.float32,
    )
    value_bias_grad = jnp.sum(grad_values.astype(jnp.float32), axis=0) + jnp.sum(
        memory_value_gradient.astype(jnp.float32), axis=(0, 1)
    )
    grad_first = lax.psum_scatter(
        (
            back_dot(grad_queries, query_weight)
            + back_dot(grad_keys, key_matrix)
            + back_dot(grad_values, value_matrix)
        ).astype(jnp.bfloat16),
        "head",
        scatter_dimension=0,
        tiled=True,
    ).astype(jnp.float32)
    first_gain_grad = jnp.sum(grad_first * normed_one, axis=0)
    first_shift_grad = jnp.sum(grad_first, axis=0)
    input_grad = (grad_hidden + norm_back(grad_first * first_gain, normed_one, factor_one)).astype(
        jnp.bfloat16
    )
    (
        query_weight_grad,
        query_bias_grad,
        key_weight_grad,
        value_weight_grad,
        value_bias_grad,
        out_weight_grad,
        centre_weight_grad,
        width_weight_grad,
        down_weight_grad,
        up_weight_grad,
        up_bias_grad,
    ) = lax.psum(
        (
            query_weight_grad,
            query_bias_grad,
            key_weight_grad,
            value_weight_grad,
            value_bias_grad,
            out_weight_grad,
            centre_weight_grad,
            width_weight_grad,
            down_weight_grad,
            up_weight_grad,
            up_bias_grad,
        ),
        "batch",
    )
    (
        first_gain_grad,
        first_shift_grad,
        out_bias_grad,
        second_gain_grad,
        second_shift_grad,
        down_bias_grad,
    ) = lax.psum(
        (
            first_gain_grad,
            first_shift_grad,
            out_bias_grad,
            second_gain_grad,
            second_shift_grad,
            down_bias_grad,
        ),
        ("batch", "head"),
    )
    return (
        layer_output,
        input_grad,
        first_gain_grad,
        first_shift_grad,
        query_weight_grad,
        query_bias_grad,
        key_weight_grad,
        value_weight_grad,
        value_bias_grad,
        out_weight_grad,
        out_bias_grad,
        second_gain_grad,
        second_shift_grad,
        up_weight_grad,
        up_bias_grad,
        down_weight_grad,
        down_bias_grad,
        centre_weight_grad,
        width_weight_grad,
    )


def solution(mesh):
    placed = (
        P(("batch", "head"), None),
        P("batch"),
        P("batch"),
        P("batch", None, None),
        P(),
        P(),
        P(None, "head"),
        P("head"),
        P(None, "head"),
        P(None, "head"),
        P("head"),
        P("head", None),
        P(),
        P(),
        P(),
        P(None, "head"),
        P("head"),
        P("head", None),
        P(),
        P("head", None),
        P("head", None),
        P(("batch", "head"), None),
    )
    return jax.shard_map(
        per_device,
        mesh=mesh,
        in_specs=placed,
        out_specs=(
            P(("batch", "head"), None),
            P(("batch", "head"), None),
            P(),
            P(),
            P(None, "head"),
            P("head"),
            P(None, "head"),
            P(None, "head"),
            P("head"),
            P("head", None),
            P(),
            P(),
            P(),
            P(None, "head"),
            P("head"),
            P("head", None),
            P(),
            P("head", None),
            P("head", None),
        ),
        check_vma=False,
    )
```

profile of v0, /device:TPU:0, one launch (start us, length us, event | category | flops | bytes accessed | tf_op | source)
XLA Modules:
  0.0 868.7 jit_solution(15008076573527793442)
XLA Ops:
  14.6 64.0 %all-gather.5.cloned.1.call-done = bf16[2048,768]{1,0:T(8,128)(2,1)} async-done(((bf16[512,768]{1,0:T(8,128)(2,1)}), bf16[2048,768]{1,0:T(8,128)(2,1)}) %all-gather.5.cloned.1.call-update) | async-done | bytes 3145744 | tf_op jit(solution)/shard_map/all_gather | solution.py:189
  78.6 3.1 fusion.166
  84.5 3.9 fusion.165
  88.4 3.1 reshape.257
  91.6 2.2 copy.58
  93.7 4.0 convolution_convert_fusion.4
  97.7 3.0 reshape.259
  100.7 2.2 copy.60
  103.9 54.4 %while.34 = (s32[]{:T(128)}, bf16[4,512,3,64]{1,3,2,0:T(8,128)(2,1)}, f32[4,3,512]{2,1,0:T(4,128)}, bf16[4,512,3,64]{1,3,2,0:T(8,128)(2,1)}, s32[4]{0:T(128)S(1)...) while((s32[]{:T(128)}, ...), condition=%wide.region_5.6_spmd, body=%wide.region_2.5_spmd.sunk | while | flops 325111296 | bytes 17297064 | solution.py:221
  111.6 2.0 fusion.318
  114.3 3.2 fusion.321
  125.2 2.0 fusion.318
  127.9 3.2 fusion.321
  138.8 2.0 fusion.318
  141.5 3.2 fusion.321
  152.4 2.0 fusion.318
  155.0 3.2 fusion.321
  161.1 2.7 convolution_convert_fusion.2
  166.4 56.4 %reduce-scatter.5.cloned.1.call-done = bf16[512,768]{1,0:T(8,128)(2,1)} async-done(((bf16[2048,768]{1,0:T(8,128)(2,1)}), bf16[512,768]{1,0:T(8,128)(2,1)}) %reduce-scatter.5.cloned.1.call-update) | async-done | bytes 786448 | tf_op jit(solution)/shard_map/reduce_scatter | solution.py:225
  228.9 61.8 %all-gather.7.cloned.1.call-done = bf16[2048,768]{1,0:T(8,128)(2,1)} async-done(((bf16[512,768]{1,0:T(8,128)(2,1)}), bf16[2048,768]{1,0:T(8,128)(2,1)}) %all-gather.7.cloned.1.call-update) | async-done | bytes 3145744 | tf_op jit(solution)/shard_map/all_gather | solution.py:234
  290.6 7.5 fusion.196
  298.1 56.1 %all-gather.9.cloned.1.call-done = bf16[2048,768]{1,0:T(8,128)(2,1)} async-done(((bf16[512,768]{1,0:T(8,128)(2,1)}), bf16[2048,768]{1,0:T(8,128)(2,1)}) %all-gather.9.cloned.1.call-update) | async-done | bytes 3145744 | tf_op jit(solution)/shard_map/all_gather | solution.py:245
  354.3 11.0 %convert_reduce_fusion = (f32[768]{0:T(1024)}, bf16[2048,768]{1,0:T(8,128)(2,1)S(1)}, bf16[2048,768]{1,0:T(8,128)(2,1)}) fusion(f32[2048,768]{1,0:T(8,128)} %fusion.196, f32[768]{0:T(1024)} %convert_element_type.193, bf16[2048,768]{1,0:T(8,128)(2,1)} %all-gather.9.cloned.1.call-done, bf16[768,768]{1,0:T(8,128)(2,1)} %param.43), kind=kOutput, calls=%fused_computation.206 | convolution fusion | flops 2455239936 | bytes 16914432 | tf_op jit(solution)/shard_map/dot_general | solution.py:29
  366.9 4.0 convolution_convert_fusion
  371.0 6.5 convolution_convert_fusion.1
  378.8 51.2 %reduce-scatter.9.cloned.1.call-done = bf16[512,768]{1,0:T(8,128)(2,1)} async-done(((bf16[2048,768]{1,0:T(8,128)(2,1)}), bf16[512,768]{1,0:T(8,128)(2,1)}) %reduce-scatter.9.cloned.1.call-update) | async-done | bytes 786448 | tf_op jit(solution)/shard_map/reduce_scatter | solution.py:252
  430.0 2.9 fusion.188
  433.5 59.0 %reduce-scatter.7.cloned.1.call-done = bf16[512,768]{1,0:T(8,128)(2,1)} async-done(((bf16[2048,768]{1,0:T(8,128)(2,1)}), bf16[512,768]{1,0:T(8,128)(2,1)}) %reduce-scatter.7.cloned.1.call-update) | async-done | bytes 786448 | tf_op jit(solution)/shard_map/reduce_scatter | solution.py:237
  492.5 5.3 convert_reduce_fusion.5
  497.8 63.6 %all-gather.11.cloned.1.call-done = bf16[2048,768]{1,0:T(8,128)(2,1)} async-done(((bf16[512,768]{1,0:T(8,128)(2,1)}), bf16[2048,768]{1,0:T(8,128)(2,1)}) %all-gather.11.cloned.1.call-update) | async-done | bytes 3145744 | tf_op jit(solution)/shard_map/all_gather | solution.py:262
  561.4 4.0 convolution_convert_fusion.3
  565.4 3.4 reshape.263
  568.8 2.2 copy.64
  573.9 91.2 %while.35 = (s32[]{:T(128)}, bf16[4,512,3,64]{1,3,2,0:T(8,128)(2,1)}, bf16[4,512,3,64]{1,3,2,0:T(8,128)(2,1)}, bf16[4,512,3,64]{1,3,2,0:T(8,128)(2,1)}, bf16[4,2...) while((s32[]{:T(128)}, ...), condition=%wide.region_17.18_spmd, body=%wide.region_13.17_spmd.sunk | while | flops 795121152 | bytes 42630428 | solution.py:266
  580.1 2.7 fusion.348
  602.8 2.7 fusion.348
  625.6 2.7 fusion.348
  648.4 2.7 fusion.348
  671.7 2.8 add_convert_fusion.3
  674.6 7.1 fusion.201
  681.7 4.2 fusion.200
  701.8 25.6 %all-reduce.1 = (f32[192]{0:T(256)}, f32[192]{0:T(256)}, f32[768]{0:T(1024)}, f32[3,256]{1,0:T(4,128)}, f32[3,256]{1,0:T(4,128)}) all-reduce(f32[192]{0:T(256)} %reduce_sum.229, f32[192]{0:T(256)S(1)} %add.258, f32[768]{0:T(1024)} %get-tuple-element.347, f32[3,256]{1,0:T(4,128)} %reduce_sum.237, ...), channel_id=1, replica_groups=mesh['batch'=8,'head'=4] {'batch'}, use_global_device_ids=true, to_apply=%region_27.28 | all-reduce | flops 2688 | bytes 21504 | tf_op jit(solution)/shard_map/psum | solution.py:317
  727.4 6.2 reduce-scatter.11.cloned.1.call-done
  733.6 2.0 fusion.189
  735.7 41.8 %all-reduce = (f32[768]{0:T(1024)}, f32[768]{0:T(1024)}, f32[768]{0:T(1024)}, f32[768]{0:T(1024)}, f32[768]{0:T(1024)}, /*index=5*/f32[768]{0:T(1024)}) all-reduce(f32[768]{0:T(1024)S(1)} %get-tuple-element.260, f32[768]{0:T(1024)S(1)} %get-tuple-element.265, ...), channel_id=1, replica_groups=mesh['batch'=8,'head'=4] {'batch','head'}, use_global_device_ids=true, to_apply=%region_22.23 | all-reduce | flops 4608 | bytes 36864 | tf_op jit(solution)/shard_map/psum | solution.py:340
  777.5 2.9 fusion.182
  780.4 73.2 %all-reduce.5.cloned.1.call-done = (f32[768,192]{0,1:T(8,128)}, f32[768,192]{0,1:T(8,128)}, f32[768,192]{0,1:T(8,128)}, f32[192,768]{1,0:T(8,128)}, f32[768,768]{1,0:T(8,128)}, /*index=5*/f32[768,768]{1,0:T(8,128)}) async-done(((f32[768,192]{0,1:T(8,128)}, f32[768,192]{0,1:T(8,128)}, f32[768,192]{0,1:T(8,128)}, f32[192,768]{1,0:T(8,128)}, f32[768,768]{1,0:T(8,128)}, /*index=5*/f32[768,768]{1,0:T(8,128)}), ...) | async-done | bytes 7077904 | tf_op jit(solution)/shard_map/psum | solution.py:317
  853.5 2.0 copy.222
  (365 shorter events, 170.6 us)
Async XLA Ops:
  7.2 5.2 copy-start
  7.2 3.8 copy-start.1
  7.2 3.1 copy-start.45
  7.2 3.2 copy-start.46
  7.2 71.4 %all-gather.5.cloned.1.call-start = ((), (), s32[]{:S(2)}) async-start(), calls=%async_computation.4 | async-start | bytes 3932160 | tf_op jit(solution)/shard_map/all_gather | solution.py:189
  8.8 3.6 copy-start.50
  8.8 3.6 copy-start.51
  8.8 3.6 copy-start.52
  8.8 3.6 copy-start.26
  12.3 210.6 %reduce-scatter.5.cloned.1.call-start = ((), (), s32[]{:S(2)}) async-start(), calls=%async_computation.5 | async-start | bytes 3932160 | tf_op jit(solution)/shard_map/reduce_scatter | solution.py:225
  100.7 3.2 copy-start.33
  100.7 3.2 copy-start.34
  100.7 3.2 copy-start.53
  158.3 2.9 copy-start.29
  163.8 126.8 %all-gather.7.cloned.1.call-start = ((), (), s32[]{:S(2)}) async-start(), calls=%async_computation.6 | async-start | bytes 3932160 | tf_op jit(solution)/shard_map/all_gather | solution.py:234
  222.9 2.7 copy-start.43
  227.0 127.3 %all-gather.9.cloned.1.call-start = ((), (), s32[]{:S(2)}) async-start(), calls=%async_computation.8 | async-start | bytes 3932160 | tf_op jit(solution)/shard_map/all_gather | solution.py:245
  227.6 202.4 %reduce-scatter.9.cloned.1.call-start = ((), (), s32[]{:S(2)}) async-start(), calls=%async_computation.9 | async-start | bytes 3932160 | tf_op jit(solution)/shard_map/reduce_scatter | solution.py:252
  354.3 12.6 %copy-start.49 = (bf16[768,768]{1,0:T(8,128)(2,1)S(1)}, bf16[768,768]{1,0:T(8,128)(2,1)}, u32[]{:S(2)}) copy-start(bf16[768,768]{1,0:T(8,128)(2,1)} %param.41) | copy-start | bytes 3538948
  370.9 121.5 %reduce-scatter.7.cloned.1.call-start = ((), (), s32[]{:S(2)}) async-start(), calls=%async_computation.7 | async-start | bytes 3932160 | tf_op jit(solution)/shard_map/reduce_scatter | solution.py:237
  377.5 183.9 %all-gather.11.cloned.1.call-start = ((), (), s32[]{:S(2)}) async-start(), calls=%async_computation.10 | async-start | bytes 3932160 | tf_op jit(solution)/shard_map/all_gather | solution.py:262
  497.8 235.9 %reduce-scatter.11.cloned.1.call-start = ((), (), s32[]{:S(2)}) async-start(), calls=%async_computation.11 | async-start | bytes 3932160 | tf_op jit(solution)/shard_map/reduce_scatter | solution.py:290
  571.0 2.9 copy-start.54
  571.0 2.9 copy-start.56
  577.1 3.0 copy-start.11
  599.8 3.0 copy-start.11
  622.6 3.0 copy-start.11
  645.4 3.0 copy-start.11
  667.2 3.5 copy-start.9
  668.0 3.7 copy-start.12
  674.5 179.0 %all-reduce.5.cloned.1.call-start = ((), (), s32[]{:S(2)}) async-start(), calls=%async_computation.12 | async-start | bytes 14155776 | tf_op jit(solution)/shard_map/psum | solution.py:317
  674.6 7.1 copy-start.48
  674.6 7.1 copy-start.58
  681.7 4.2 copy-start.25
  685.9 2.1 copy-start.16
  688.2 2.1 copy-start.2
  688.2 2.3 copy-start.10
  695.3 6.1 copy-start.15
  695.3 38.3 %copy-start.36 = (f32[768]{0:T(1024)S(1)}, f32[768]{0:T(1024)}, u32[]{:S(2)}) copy-start(f32[768]{0:T(1024)} %copy-done.35) | copy-start | bytes 9220
  695.4 38.3 %copy-start.38 = (f32[512]{0:T(512)S(1)}, f32[512]{0:T(512)}, u32[]{:S(2)}) copy-start(f32[512]{0:T(512)} %copy-done.37) | copy-start | bytes 6148
  695.4 38.3 %copy-start.41 = (f32[512]{0:T(512)S(1)}, f32[512]{0:T(512)}, u32[]{:S(2)}) copy-start(f32[512]{0:T(512)} %copy-done.40) | copy-start | bytes 6148
  700.0 35.7 %copy-start.44 = (f32[768]{0:T(1024)S(1)}, f32[768]{0:T(1024)}, u32[]{:S(2)}) copy-start(f32[768]{0:T(1024)} %get-tuple-element.258) | copy-start | bytes 9220
  733.6 43.9 %copy-start.18 = (bf16[512,768]{1,0:T(8,128)(2,1)S(1)}, bf16[512,768]{1,0:T(8,128)(2,1)}, u32[]{:S(2)}) copy-start(bf16[512,768]{1,0:T(8,128)(2,1)} %reduce-scatter.11.cloned.1.call-done) | copy-start | bytes 2359300
  853.5 2.1 copy-start.24
  853.5 2.9 copy-start.23
  853.5 3.7 copy-start.22
  855.6 2.5 copy-start.20
  858.0 2.5 copy-start.19
  (26 other events, 33.4 us)
Sparse Core Ops, SparseCore 0:
  12.4 66.1 all-gather.4
  163.9 58.8 reduce-scatter.4
  227.1 63.5 all-gather.6
  292.1 62.1 all-gather.8
  371.0 58.8 reduce-scatter.8
  432.1 60.2 reduce-scatter.6
  497.9 63.5 all-gather.10
  674.7 58.8 reduce-scatter.10
  738.8 114.6 all-reduce.4
where the time goes:
time: 874 us; the launch traced here: 869 us
  waiting for transfers between devices  492 us (56%)
  matrix products  186 us (21%)
  blocking collectives  67.4 us (8%)
  local copies, waits for them, and re-layouts  60 us (7%)
  other arithmetic  46.6 us (5%)
  between operations  14.6 us (2%)
    psum x1, waiting for transfers between devices, per_device(): lax.psum((query_weight_grad, query_bias_grad, key_weight_grad, value_weig...  73.2 us
    all_gather x1, waiting for transfers between devices, per_device(): first_rows = lax.all_gather(first_low, 'head', axis=0, tiled=True)  64 us
    all_gather x1, waiting for transfers between devices, per_device(): branch_rows = lax.all_gather(branch_low, 'head', axis=0, tiled=True)  63.6 us
    all_gather x1, waiting for transfers between devices, per_device(): second_rows = lax.all_gather(second_low, 'head', axis=0, tiled=True)  61.8 us
    reduce_scatter x1, waiting for transfers between devices, per_device(): lax.psum_scatter(jnp.dot(up_act, down_weight, preferred_element_type=jnp....  59 us
    reduce_scatter x1, waiting for transfers between devices, per_device(): lax.psum_scatter(jnp.dot(context, out_weight, preferred_element_type=jnp....  56.4 us
    all_gather x1, waiting for transfers between devices, per_device(): grad_rows = lax.all_gather(grad_output, 'head', axis=0, tiled=True)  56.1 us
    reduce_scatter x1, waiting for transfers between devices, per_device(): lax.psum_scatter(back_dot(grad_up, up_weight).astype(jnp.bfloat16), 'head...  51.2 us
  transfers between devices with their start and end apart: 9, of which 9 were waited for; matrix products, arithmetic and copies ran while one was open for 6% of the time, Pallas kernels for 0%

commit v1 on v0

--- a/solution.py
+++ b/solution.py
@@ -337,16 +337,19 @@
         second_gain_grad,
         second_shift_grad,
         down_bias_grad,
-    ) = lax.psum(
-        (
-            first_gain_grad,
-            first_shift_grad,
-            out_bias_grad,
-            second_gain_grad,
-            second_shift_grad,
-            down_bias_grad,
+    ) = jax.lax.psum(
+        jax.lax.psum(
+            (
+                first_gain_grad,
+                first_shift_grad,
+                out_bias_grad,
+                second_gain_grad,
+                second_shift_grad,
+                down_bias_grad,
+            ),
+            "head",
         ),
-        ("batch", "head"),
+        "batch",
     )
     return (
         layer_output,

time: 874 us -> 874 us (level)
  waiting for transfers between devices: 492 us -> 516 us
  blocking collectives: 67.4 us -> 44.2 us
    reduce_scatter x1, waiting for transfers between devices: 6.24 us -> 31.8 us  [per_device(): lax.psum_scatter((back_dot(grad_queries, query_weight) + back_dot(grad_ke...]
    psum x2, blocking collectives: 67.4 us -> 44.2 us  [the longest x1 25.8 us: per_device(): jax.lax.psum(jax.lax.psum((first_gain_grad, first_shift_grad, out_bias_gr...]
where the time goes in v1:
time: 874 us; the launch traced here: 869 us
  waiting for transfers between devices  516 us (59%)
  matrix products  186 us (21%)
  local copies, waits for them, and re-layouts  60 us (7%)
  other arithmetic  46.6 us (5%)
  blocking collectives  44.2 us (5%)
  between operations  14.7 us (2%)
    psum x1, waiting for transfers between devices, per_device(): lax.psum((query_weight_grad, query_bias_grad, key_weight_grad, value_weig...  71.1 us
    all_gather x1, waiting for transfers between devices, per_device(): first_rows = lax.all_gather(first_low, 'head', axis=0, tiled=True)  64 us
    all_gather x1, waiting for transfers between devices, per_device(): branch_rows = lax.all_gather(branch_low, 'head', axis=0, tiled=True)  63.6 us
    all_gather x1, waiting for transfers between devices, per_device(): second_rows = lax.all_gather(second_low, 'head', axis=0, tiled=True)  61.8 us
    reduce_scatter x1, waiting for transfers between devices, per_device(): lax.psum_scatter(jnp.dot(up_act, down_weight, preferred_element_type=jnp....  59 us
    reduce_scatter x1, waiting for transfers between devices, per_device(): lax.psum_scatter(jnp.dot(context, out_weight, preferred_element_type=jnp....  56.4 us
    all_gather x1, waiting for transfers between devices, per_device(): grad_rows = lax.all_gather(grad_output, 'head', axis=0, tiled=True)  56.1 us
    reduce_scatter x1, waiting for transfers between devices, per_device(): lax.psum_scatter(back_dot(grad_up, up_weight).astype(jnp.bfloat16), 'head...  51.2 us
  transfers between devices with their start and end apart: 9, of which 9 were waited for; matrix products, arithmetic and copies ran while one was open for 6% of the time, Pallas kernels for 0%

profile of v1, /device:TPU:0, one launch (start us, length us, event | category | flops | bytes accessed | tf_op | source)
XLA Modules:
  0.0 868.9 jit_solution(14680006970240782889)
XLA Ops:
  14.6 64.0 %all-gather.5.cloned.1.call-done = bf16[2048,768]{1,0:T(8,128)(2,1)} async-done(((bf16[512,768]{1,0:T(8,128)(2,1)}), bf16[2048,768]{1,0:T(8,128)(2,1)}) %all-gather.5.cloned.1.call-update) | async-done | bytes 3145744 | tf_op jit(solution)/shard_map/all_gather | solution.py:189
  78.6 3.1 fusion.166
  84.5 3.9 fusion.165
  88.4 3.1 reshape.257
  91.6 2.2 copy.58
  93.7 4.0 convolution_convert_fusion.4
  97.7 3.0 reshape.259
  100.7 2.2 copy.60
  103.9 54.4 %while.34 = (s32[]{:T(128)}, bf16[4,512,3,64]{1,3,2,0:T(8,128)(2,1)}, f32[4,3,512]{2,1,0:T(4,128)}, bf16[4,512,3,64]{1,3,2,0:T(8,128)(2,1)}, s32[4]{0:T(128)S(1)...) while((s32[]{:T(128)}, ...), condition=%wide.region_5.6_spmd, body=%wide.region_2.5_spmd.sunk | while | flops 325111296 | bytes 17297064 | solution.py:221
  111.6 2.0 fusion.318
  114.3 3.2 fusion.321
  125.2 2.0 fusion.318
  127.9 3.2 fusion.321
  138.8 2.0 fusion.318
  141.5 3.2 fusion.321
  152.4 2.0 fusion.318
  155.0 3.2 fusion.321
  161.1 2.7 convolution_convert_fusion.2
  166.5 56.4 %reduce-scatter.5.cloned.1.call-done = bf16[512,768]{1,0:T(8,128)(2,1)} async-done(((bf16[2048,768]{1,0:T(8,128)(2,1)}), bf16[512,768]{1,0:T(8,128)(2,1)}) %reduce-scatter.5.cloned.1.call-update) | async-done | bytes 786448 | tf_op jit(solution)/shard_map/reduce_scatter | solution.py:225
  228.9 61.8 %all-gather.7.cloned.1.call-done = bf16[2048,768]{1,0:T(8,128)(2,1)} async-done(((bf16[512,768]{1,0:T(8,128)(2,1)}), bf16[2048,768]{1,0:T(8,128)(2,1)}) %all-gather.7.cloned.1.call-update) | async-done | bytes 3145744 | tf_op jit(solution)/shard_map/all_gather | solution.py:234
  290.7 7.5 fusion.196
  298.2 56.1 %all-gather.9.cloned.1.call-done = bf16[2048,768]{1,0:T(8,128)(2,1)} async-done(((bf16[512,768]{1,0:T(8,128)(2,1)}), bf16[2048,768]{1,0:T(8,128)(2,1)}) %all-gather.9.cloned.1.call-update) | async-done | bytes 3145744 | tf_op jit(solution)/shard_map/all_gather | solution.py:245
  354.3 11.0 %convert_reduce_fusion = (f32[768]{0:T(1024)}, bf16[2048,768]{1,0:T(8,128)(2,1)S(1)}, bf16[2048,768]{1,0:T(8,128)(2,1)}) fusion(f32[2048,768]{1,0:T(8,128)} %fusion.196, f32[768]{0:T(1024)} %convert_element_type.193, bf16[2048,768]{1,0:T(8,128)(2,1)} %all-gather.9.cloned.1.call-done, bf16[768,768]{1,0:T(8,128)(2,1)} %param.43), kind=kOutput, calls=%fused_computation.206 | convolution fusion | flops 2455239936 | bytes 16914432 | tf_op jit(solution)/shard_map/dot_general | solution.py:29
  366.9 4.0 convolution_convert_fusion
  371.0 6.5 convolution_convert_fusion.1
  378.8 51.2 %reduce-scatter.9.cloned.1.call-done = bf16[512,768]{1,0:T(8,128)(2,1)} async-done(((bf16[2048,768]{1,0:T(8,128)(2,1)}), bf16[512,768]{1,0:T(8,128)(2,1)}) %reduce-scatter.9.cloned.1.call-update) | async-done | bytes 786448 | tf_op jit(solution)/shard_map/reduce_scatter | solution.py:252
  430.0 2.9 fusion.188
  433.5 59.0 %reduce-scatter.7.cloned.1.call-done = bf16[512,768]{1,0:T(8,128)(2,1)} async-done(((bf16[2048,768]{1,0:T(8,128)(2,1)}), bf16[512,768]{1,0:T(8,128)(2,1)}) %reduce-scatter.7.cloned.1.call-update) | async-done | bytes 786448 | tf_op jit(solution)/shard_map/reduce_scatter | solution.py:237
  492.5 5.3 convert_reduce_fusion.5
  497.9 63.6 %all-gather.11.cloned.1.call-done = bf16[2048,768]{1,0:T(8,128)(2,1)} async-done(((bf16[512,768]{1,0:T(8,128)(2,1)}), bf16[2048,768]{1,0:T(8,128)(2,1)}) %all-gather.11.cloned.1.call-update) | async-done | bytes 3145744 | tf_op jit(solution)/shard_map/all_gather | solution.py:262
  561.4 4.0 convolution_convert_fusion.3
  565.4 3.4 reshape.263
  568.8 2.2 copy.64
  573.9 91.2 %while.35 = (s32[]{:T(128)}, bf16[4,512,3,64]{1,3,2,0:T(8,128)(2,1)}, bf16[4,512,3,64]{1,3,2,0:T(8,128)(2,1)}, bf16[4,512,3,64]{1,3,2,0:T(8,128)(2,1)}, bf16[4,2...) while((s32[]{:T(128)}, ...), condition=%wide.region_17.18_spmd, body=%wide.region_13.17_spmd.sunk | while | flops 795121152 | bytes 42630428 | solution.py:266
  580.1 2.7 fusion.348
  602.8 2.7 fusion.348
  625.6 2.7 fusion.348
  648.3 2.7 fusion.348
  671.7 2.8 add_convert_fusion.3
  674.5 7.1 fusion.201
  681.6 4.2 fusion.200
  701.7 31.8 %reduce-scatter.11.cloned.1.call-done = bf16[512,768]{1,0:T(8,128)(2,1)} async-done(((bf16[2048,768]{1,0:T(8,128)(2,1)}), bf16[512,768]{1,0:T(8,128)(2,1)}) %reduce-scatter.11.cloned.1.call-update) | async-done | bytes 786448 | tf_op jit(solution)/shard_map/reduce_scatter | solution.py:290
  733.6 2.0 fusion.189
  735.6 18.4 %all-reduce.2 = (f32[768]{0:T(1024)S(1)}, f32[768]{0:T(1024)S(1)}, f32[768]{0:T(1024)S(1)}, f32[768]{0:T(1024)S(1)}, f32[768]{0:T(1024)S(1)}, /*index=5*/f32[768]{0:T(1024)S(1)}) all-reduce(f32[768]{0:T(1024)S(1)} %get-tuple-element.260, f32[768]{0:T(1024)S(1)} %get-tuple-element.265, ...), channel_id=1, replica_groups=mesh['batch'=8,'head'=4] {'head'}, use_global_device_ids=true, to_apply=%region_22.23 | all-reduce | flops 4608 | bytes 36864 | tf_op jit(solution)/shard_map/psum | solution.py:341
  754.0 25.8 %all-reduce = (f32[768]{0:T(1024)}, f32[768]{0:T(1024)}, f32[192]{0:T(256)}, f32[192]{0:T(256)}, f32[768]{0:T(1024)}, /*index=5*/f32[768]{0:T(1024)}, f32[768]{0...) all-reduce(f32[768]{0:T(1024)S(1)} %get-tuple-element.345, ...), channel_id=1, replica_groups=mesh['batch'=8,'head'=4] {'batch'}, use_global_device_ids=true, to_apply=%region_23.24 | all-reduce | flops 7296 | bytes 58368 | tf_op jit(solution)/shard_map/psum | solution.py:340
  779.8 2.9 fusion.182
  782.7 71.1 %all-reduce.5.cloned.1.call-done = (f32[768,192]{0,1:T(8,128)}, f32[768,192]{0,1:T(8,128)}, f32[768,192]{0,1:T(8,128)}, f32[192,768]{1,0:T(8,128)}, f32[768,768]{1,0:T(8,128)}, /*index=5*/f32[768,768]{1,0:T(8,128)}) async-done(((f32[768,192]{0,1:T(8,128)}, f32[768,192]{0,1:T(8,128)}, f32[768,192]{0,1:T(8,128)}, f32[192,768]{1,0:T(8,128)}, f32[768,768]{1,0:T(8,128)}, /*index=5*/f32[768,768]{1,0:T(8,128)}), ...) | async-done | bytes 7077904 | tf_op jit(solution)/shard_map/psum | solution.py:317
  853.8 2.0 copy.222
  (367 shorter events, 170.6 us)
Async XLA Ops:
  7.2 5.2 copy-start
  7.2 3.8 copy-start.1
  7.2 3.1 copy-start.46
  7.2 3.2 copy-start.47
  7.2 71.4 %all-gather.5.cloned.1.call-start = ((), (), s32[]{:S(2)}) async-start(), calls=%async_computation.4 | async-start | bytes 3932160 | tf_op jit(solution)/shard_map/all_gather | solution.py:189
  8.8 3.6 copy-start.51
  8.8 3.6 copy-start.52
  8.8 3.6 copy-start.53
  8.8 3.6 copy-start.26
  12.3 210.6 %reduce-scatter.5.cloned.1.call-start = ((), (), s32[]{:S(2)}) async-start(), calls=%async_computation.5 | async-start | bytes 3932160 | tf_op jit(solution)/shard_map/reduce_scatter | solution.py:225
  100.7 3.2 copy-start.33
  100.7 3.2 copy-start.34
  100.7 3.2 copy-start.54
  158.3 2.9 copy-start.29
  163.8 126.8 %all-gather.7.cloned.1.call-start = ((), (), s32[]{:S(2)}) async-start(), calls=%async_computation.6 | async-start | bytes 3932160 | tf_op jit(solution)/shard_map/all_gather | solution.py:234
  222.9 2.7 copy-start.43
  227.0 127.3 %all-gather.9.cloned.1.call-start = ((), (), s32[]{:S(2)}) async-start(), calls=%async_computation.8 | async-start | bytes 3932160 | tf_op jit(solution)/shard_map/all_gather | solution.py:245
  227.6 202.4 %reduce-scatter.9.cloned.1.call-start = ((), (), s32[]{:S(2)}) async-start(), calls=%async_computation.9 | async-start | bytes 3932160 | tf_op jit(solution)/shard_map/reduce_scatter | solution.py:252
  354.3 12.6 %copy-start.50 = (bf16[768,768]{1,0:T(8,128)(2,1)S(1)}, bf16[768,768]{1,0:T(8,128)(2,1)}, u32[]{:S(2)}) copy-start(bf16[768,768]{1,0:T(8,128)(2,1)} %param.41) | copy-start | bytes 3538948
  370.9 121.5 %reduce-scatter.7.cloned.1.call-start = ((), (), s32[]{:S(2)}) async-start(), calls=%async_computation.7 | async-start | bytes 3932160 | tf_op jit(solution)/shard_map/reduce_scatter | solution.py:237
  377.5 183.9 %all-gather.11.cloned.1.call-start = ((), (), s32[]{:S(2)}) async-start(), calls=%async_computation.10 | async-start | bytes 3932160 | tf_op jit(solution)/shard_map/all_gather | solution.py:262
  497.8 235.8 %reduce-scatter.11.cloned.1.call-start = ((), (), s32[]{:S(2)}) async-start(), calls=%async_computation.11 | async-start | bytes 3932160 | tf_op jit(solution)/shard_map/reduce_scatter | solution.py:290
  571.0 2.9 copy-start.55
  571.0 2.9 copy-start.57
  577.1 3.0 copy-start.11
  599.8 3.0 copy-start.11
  622.6 3.0 copy-start.11
  645.4 3.0 copy-start.11
  667.1 3.5 copy-start.9
  667.9 3.7 copy-start.12
  674.5 179.3 %all-reduce.5.cloned.1.call-start = ((), (), s32[]{:S(2)}) async-start(), calls=%async_computation.12 | async-start | bytes 14155776 | tf_op jit(solution)/shard_map/psum | solution.py:317
  674.5 7.1 copy-start.49
  674.5 7.1 copy-start.59
  681.6 4.2 copy-start.25
  685.8 2.1 copy-start.16
  688.1 2.1 copy-start.2
  688.1 2.3 copy-start.10
  695.3 6.1 copy-start.15
  695.3 38.3 %copy-start.36 = (f32[768]{0:T(1024)S(1)}, f32[768]{0:T(1024)}, u32[]{:S(2)}) copy-start(f32[768]{0:T(1024)} %copy-done.35) | copy-start | bytes 9220
  695.3 38.3 %copy-start.38 = (f32[512]{0:T(512)S(1)}, f32[512]{0:T(512)}, u32[]{:S(2)}) copy-start(f32[512]{0:T(512)} %copy-done.37) | copy-start | bytes 6148
  695.3 38.3 %copy-start.41 = (f32[512]{0:T(512)S(1)}, f32[512]{0:T(512)}, u32[]{:S(2)}) copy-start(f32[512]{0:T(512)} %copy-done.40) | copy-start | bytes 6148
  699.9 35.7 %copy-start.44 = (f32[768]{0:T(1024)S(1)}, f32[768]{0:T(1024)}, u32[]{:S(2)}) copy-start(f32[768]{0:T(1024)} %get-tuple-element.258) | copy-start | bytes 9220
  701.4 52.6 %copy-start.45 = (f32[192]{0:T(256)S(1)}, f32[192]{0:T(256)}, u32[]{:S(2)}) copy-start(f32[192]{0:T(256)} %reduce_sum.229) | copy-start | bytes 2308
  733.6 46.3 %copy-start.18 = (bf16[512,768]{1,0:T(8,128)(2,1)S(1)}, bf16[512,768]{1,0:T(8,128)(2,1)}, u32[]{:S(2)}) copy-start(bf16[512,768]{1,0:T(8,128)(2,1)} %reduce-scatter.11.cloned.1.call-done) | copy-start | bytes 2359300
  853.8 2.9 copy-start.23
  853.8 3.7 copy-start.22
  855.8 2.5 copy-start.20
  858.3 2.5 copy-start.19
  (27 other events, 35.5 us)
Sparse Core Ops, SparseCore 0:
  12.4 66.1 all-gather.4
  164.0 58.8 reduce-scatter.4
  227.1 63.5 all-gather.6
  292.1 62.1 all-gather.8
  371.0 58.8 reduce-scatter.8
  432.1 60.2 reduce-scatter.6
  497.9 63.5 all-gather.10
  674.6 58.8 reduce-scatter.10
  738.8 114.9 all-reduce.4
